TPU v7x, 512 devices: a whole 4x8x8 slice. The times are simulated.
512 devices in a mesh: expert: 64 (over z, y), tensor: 8 (over x, core).
Axes of the slice: x: 4, y: 8, z: 8, core: 2. Of those that a mesh axis runs over, the one named last changes fastest.
Arguments:
- attn_out: bfloat16 [8192, 4096], P('expert', 'tensor'), may hold values from -6 to 6
- out_weight: bfloat16 [4096, 2048], P('tensor'), may hold values from -0.09375 to 0.09375
- residual: bfloat16 [8192, 2048], P(('expert', 'tensor')), may hold values from -6 to 6
- attn_gain: float32 [2048], replicated, may hold values from 0.1 to 1.9
- expert_ids: int32 [8192, 8], P('expert'), may hold values from 0 to 127, all different within a row; in each aligned block of 128 rows (0 to 127, 128 to 255, ...) at most 12 rows name the same one
- route_weights: float32 [8192, 8], P('expert'), may hold values from 0.05 to 0.3
- w_gate: bfloat16 [64, 2048, 1536], P('expert', None, 'tensor'), may hold values from -0.125 to 0.125
- w_up: bfloat16 [64, 2048, 1536], P('expert', None, 'tensor'), may hold values from -0.125 to 0.125
- w_down: bfloat16 [64, 1536, 2048], P('expert', 'tensor'), may hold values from -0.21875 to 0.21875
- input_gain: float32 [2048], replicated, may hold values from 0.1 to 1.9
- q_weight: bfloat16 [2048, 4096], P('expert', 'tensor'), may hold values from -0.125 to 0.125
- kv_weight: bfloat16 [2048, 1024], P('expert', 'tensor'), may hold values from -0.125 to 0.125
- q_gain: float32 [128], replicated, may hold values from 0.1 to 1.9
- k_gain: float32 [128], replicated, may hold values from 0.1 to 1.9
Outputs:
- next_residual: bfloat16 [8192, 2048], P(('expert', 'tensor'))
- queries: bfloat16 [8192, 4096], P('expert', 'tensor')
- keys_values: bfloat16 [8192, 1024], P('expert', 'tensor')
Inputs may be any that keep to these rules, and one draw needn't show every extreme that they name: `expert_ids`: each row names 8 different experts. In each aligned block of 128 rows no expert is named by more than 12 rows, and in some block one expert is named by exactly 12 rows.
All inputs are finite; a program needn't handle non-finite values.
Results may differ from a plain program's by a relative error of at most 0.012.
Values may be sent and summed in bfloat16 or wider, within the bound.
A program may use at most 64 MiB of HBM per device.

v0:
```python
import jax
import jax.numpy as jnp
from jax import lax
from jax.sharding import PartitionSpec as P

KV_HEADS = 4
TOP = 8
EPSILON = 1e-06


def normalize(values, gain):
    return values * lax.rsqrt(jnp.mean(values * values, axis=-1, keepdims=True) + EPSILON) * gain


def per_device(
    attn_out,
    out_weight,
    residual,
    attn_gain,
    expert_ids,
    route_weights,
    w_gate,
    w_up,
    w_down,
    input_gain,
    q_weight,
    kv_weight,
    q_gain,
    k_gain,
):
    n_expert = lax.axis_size("expert")
    n_tensor = lax.axis_size("tensor")
    share = n_tensor // 2
    tensor_index = lax.axis_index("tensor")
    group_rows = attn_out.shape[0]
    width = residual.shape[1]
    half = tensor_index // share
    capacity = 3 * group_rows * TOP // (4 * n_expert)
    all_experts = 2 * n_expert
    attn_rows = lax.psum_scatter(
        jnp.dot(attn_out, out_weight, preferred_element_type=jnp.float32),
        "tensor",
        scatter_dimension=0,
        tiled=True,
    )
    first_residual = (residual.astype(jnp.float32) + attn_rows).astype(jnp.bfloat16)
    normed = normalize(first_residual.astype(jnp.float32), attn_gain).astype(jnp.bfloat16)
    group_normed = lax.all_gather(normed, "tensor", axis=0, tiled=True)
    flat_ids = expert_ids.reshape(-1)
    onehot = (flat_ids[:, None] == jnp.arange(all_experts, dtype=jnp.int32)[None, :]).astype(
        jnp.int32
    )
    earlier = jnp.cumsum(onehot, axis=0) - onehot
    rank = jnp.sum(earlier * onehot, axis=1)
    dest = flat_ids * capacity + rank
    row_owner = jnp.arange(flat_ids.shape[0], dtype=jnp.int32) // TOP
    slot_row = jnp.full((all_experts * capacity,), group_rows, jnp.int32).at[dest].set(row_owner)
    slot_weight = (
        jnp.zeros((all_experts * capacity,), jnp.float32).at[dest].set(route_weights.reshape(-1))
    )
    own_slots = lax.dynamic_index_in_dim(
        slot_row.reshape(n_expert, 2, capacity), half, 1, keepdims=False
    )
    own_weights = lax.dynamic_index_in_dim(
        slot_weight.reshape(n_expert, 2, capacity), half, 1, keepdims=False
    )
    padded_rows = jnp.concatenate([group_normed, jnp.zeros((1, width), jnp.bfloat16)], axis=0)
    gate_w = w_gate[0]
    up_w = w_up[0]
    down_w = w_down[0]
    outgoing = jnp.take(padded_rows, own_slots, axis=0)
    arrived = lax.all_to_all(outgoing, "expert", split_axis=0, concat_axis=0, tiled=True)
    flat = arrived.reshape(-1, width)
    gate = jnp.dot(flat, gate_w, preferred_element_type=jnp.float32)
    up = jnp.dot(flat, up_w, preferred_element_type=jnp.float32)
    act = (jax.nn.silu(gate) * up).astype(jnp.bfloat16)
    part = jnp.dot(act, down_w, preferred_element_type=jnp.float32).astype(jnp.bfloat16)
    send_part = part.reshape(arrived.shape)
    returned = lax.all_to_all(send_part, "expert", split_axis=0, concat_axis=0, tiled=True)
    weighted = own_weights.reshape(-1)[:, None] * returned.reshape(-1, width).astype(jnp.float32)
    term = (
        jnp.zeros((group_rows + 1, width), jnp.float32)
        .at[own_slots.reshape(-1)]
        .add(weighted)[:group_rows]
    )
    expert_sum = lax.psum_scatter(
        term.astype(jnp.bfloat16), "tensor", scatter_dimension=0, tiled=True
    ).astype(jnp.float32)
    next_residual = (first_residual.astype(jnp.float32) + expert_sum).astype(jnp.bfloat16)
    own_normed = normalize(next_residual.astype(jnp.float32), input_gain).astype(jnp.bfloat16)
    next_normed = lax.all_gather(own_normed, "tensor", axis=0, tiled=True)
    query_cols = q_weight.shape[1]
    kv_cols = kv_weight.shape[1]
    query_raw = jnp.dot(
        next_normed,
        lax.all_gather(q_weight, "expert", axis=0, tiled=True),
        preferred_element_type=jnp.float32,
    )
    kv_raw = jnp.dot(
        next_normed,
        lax.all_gather(kv_weight, "expert", axis=0, tiled=True),
        preferred_element_type=jnp.float32,
    )
    head_size = q_gain.shape[0]
    queries = (
        normalize(query_raw.reshape(group_rows, -1, head_size), q_gain)
        .reshape(group_rows, query_cols)
        .astype(jnp.bfloat16)
    )
    heads_here = kv_cols // head_size
    head_number = tensor_index * heads_here + jnp.arange(heads_here, dtype=jnp.int32)
    is_key = head_number < KV_HEADS
    kv_shaped = kv_raw.reshape(group_rows, heads_here, head_size)
    keys_values = (
        jnp.where(is_key[None, :, None], normalize(kv_shaped, k_gain), kv_shaped)
        .reshape(group_rows, kv_cols)
        .astype(jnp.bfloat16)
    )
    return (next_residual, queries, keys_values)


def solution(mesh):
    return jax.shard_map(
        per_device,
        mesh=mesh,
        in_specs=(
            P("expert", "tensor"),
            P("tensor", None),
            P(("expert", "tensor"), None),
            P(),
            P("expert", None),
            P("expert", None),
            P("expert", None, "tensor"),
            P("expert", None, "tensor"),
            P("expert", "tensor", None),
            P(),
            P("expert", "tensor"),
            P("expert", "tensor"),
            P(),
            P(),
        ),
        out_specs=(P(("expert", "tensor"), None), P("expert", "tensor"), P("expert", "tensor")),
        check_vma=False,
    )
```

profile of v0, /device:TPU:2, one launch (start us, length us, event | category | flops | bytes accessed | tf_op | source)
XLA Modules:
  0.0 475.3 jit_solution(3789116620057749564)
XLA Ops:
  8.1 1.5 copy-done
  9.6 2.3 fusion.42
  12.0 0.1 copy.34
  12.3 0.1 copy.33
  12.4 0.1 mul.128
  12.5 0.1 copy.36
  12.6 0.2 fusion.17
  12.9 0.1 copy.37
  13.0 0.4 fusion.16
  13.4 4.3 scatter_custom_fusion
  17.7 0.1 reshape.200
  17.9 0.5 broadcast.190
  18.4 0.7 fusion.40
  19.3 32.0 %reduce-scatter.3.cloned.1.call-done = f32[16,2048]{1,0:T(8,128)} async-done(((f32[128,2048]{1,0:T(8,128)}), f32[16,2048]{1,0:T(8,128)}) %reduce-scatter.3.cloned.1.call-update) | async-done | bytes 131088 | tf_op jit(solution)/shard_map/reduce_scatter | solution.py:40
  51.3 1.0 fusion.26
  52.4 13.8 %all_gather.12 = bf16[128,2048]{1,0:T(8,128)(2,1)S(1)} all-gather(bf16[16,2048]{1,0:T(8,128)(2,1)S(1)} %fusion.28), channel_id=1, replica_groups=mesh['expert'=64,'tensor'=8] {'tensor'}, dimensions={0}, use_global_device_ids=true | all-gather | bytes 589824 | tf_op jit(solution)/shard_map/all_gather | solution.py:48
  66.3 4.3 gather_fusion
  70.6 6.1 %reshape.208 = bf16[64,12,2048]{2,1,0:T(8,128)(2,1)} reshape(bf16[768,2048]{1,0:T(8,128)(2,1)} %gather_fusion) | data formatting | bytes 6291456 | tf_op jit(solution)/shard_map/jit(_take)/gather | solution.py:71
  76.6 2.6 broadcast_select_fusion
  79.3 111.8 %all_to_all.10 = bf16[64,12,2048]{2,1,0:T(8,128)(2,1)} all-to-all(bf16[64,12,2048]{2,1,0:T(8,128)(2,1)S(1)} %broadcast_select_fusion), channel_id=1, replica_groups=mesh['expert'=64,'tensor'=8] {'expert'}, dimensions={0} | all-to-all | bytes 6291456 | tf_op jit(solution)/shard_map/all_to_all | solution.py:72
  191.1 6.2 %reshape.204 = bf16[768,2048]{1,0:T(8,128)(2,1)} reshape(bf16[64,12,2048]{2,1,0:T(8,128)(2,1)} %all_to_all.10) | data formatting | bytes 6291456 | tf_op jit(solution)/shard_map/reshape | solution.py:73
  197.3 3.3 fusion.7
  200.5 6.5 %convolution_convert_fusion = bf16[768,2048]{1,0:T(8,128)(2,1)} fusion(bf16[768,2048]{1,0:T(8,128)(2,1)} %reshape.204, bf16[1,192,2048]{2,1,0:T(8,128)(2,1)} %param.22, bf16[1,2048,192]{1,2,0:T(8,128)(2,1)} %param.21, f32[768,192]{0,1:T(8,128)S(1)} %fusion.7), kind=kOutput, calls=%fused_computation.7 | convolution fusion | flops 1210417152 | bytes 8454144 | tf_op jit(solution)/shard_map/dot_general | solution.py:77
  207.0 6.1 %reshape.205 = bf16[64,12,2048]{2,1,0:T(8,128)(2,1)} reshape(bf16[768,2048]{1,0:T(8,128)(2,1)} %convolution_convert_fusion) | data formatting | bytes 6291456 | tf_op jit(solution)/shard_map/reshape | solution.py:78
  213.1 12.7 %all-to-all-start.1 = ((bf16[64,12,2048]{2,1,0:T(8,128)(2,1)}), bf16[64,12,2048]{2,1,0:T(8,128)(2,1)}, u32[]{:S(2)}, u32[]{:S(2)}) async-start(bf16[64,12,2048]{2,1,0:T(8,128)(2,1)} %reshape.205), calls=%async_computation.2 | async-start | bytes 8388608 | tf_op jit(solution)/shard_map/all_to_all | solution.py:79
  225.9 0.1 reshape.201
  226.0 0.1 copy.38
  226.2 4.5 scatter_custom_fusion.1
  230.7 0.1 reshape.203
  230.9 0.1 dynamic-slice_reduce_fusion
  231.0 0.1 mul.130
  231.1 96.7 %all-to-all-done.1 = bf16[64,12,2048]{2,1,0:T(8,128)(2,1)} async-done(((bf16[64,12,2048]{2,1,0:T(8,128)(2,1)}), bf16[64,12,2048]{2,1,0:T(8,128)(2,1)}, u32[]{:S(2)}, u32[]{:S(2)}) %all-to-all-start.1) | async-done | bytes 3145760 | tf_op jit(solution)/shard_map/all_to_all | solution.py:79
  327.8 6.7 %reshape.206 = f32[768,2048]{1,0:T(8,128)} reshape(bf16[64,12,2048]{2,1,0:T(8,128)(2,1)} %all-to-all-done.1) | data formatting | bytes 9437184 | tf_op jit(solution)/shard_map/convert_element_type | solution.py:80
  334.5 15.8 %scatter_custom_fusion.2 = f32[129,2048]{1,0:T(8,128)S(1)} fusion(s32[768]{0:T(1024)S(1)} %fusion.37, f32[768,2048]{1,0:T(8,128)} %reshape.206, f32[768]{0:T(1024)S(1)} %mul.130, f32[]{:T(128)} %constant.76.clone.1), kind=kCustom, calls=%fused_computation.4 | custom fusion | flops 3145728 | bytes 7352324 | tf_op jit(solution)/shard_map/scatter-add | solution.py:84
  350.3 0.9 slice.20
  351.2 0.5 all-gather.2.cloned.1.call-update
  351.7 72.7 %all_gather.15 = bf16[2048,128]{1,0:T(8,128)(2,1)S(1)} all-gather(bf16[32,128]{1,0:T(8,128)(2,1)S(1)} %copy-done.4), channel_id=1, replica_groups=mesh['expert'=64,'tensor'=8] {'expert'}, dimensions={0}, use_global_device_ids=true | all-gather | bytes 532480 | tf_op jit(solution)/shard_map/all_gather | solution.py:101
  424.5 1.0 fusion.23
  425.6 13.1 %all_gather.13 = bf16[128,2048]{1,0:T(8,128)(2,1)S(1)} all-gather(bf16[16,2048]{1,0:T(8,128)(2,1)S(1)} %fusion.25), channel_id=1, replica_groups=mesh['expert'=64,'tensor'=8] {'tensor'}, dimensions={0}, use_global_device_ids=true | all-gather | bytes 589824 | tf_op jit(solution)/shard_map/all_gather | solution.py:91
  438.7 19.9 %all-gather.2.cloned.1.call-done = bf16[2048,512]{1,0:T(8,128)(2,1)} async-done(((bf16[32,512]{1,0:T(8,128)(2,1)}), bf16[2048,512]{1,0:T(8,128)(2,1)}) %all-gather.2.cloned.1.call-update) | async-done | bytes 2097168 | tf_op jit(solution)/shard_map/all_gather | solution.py:96
  458.6 2.8 fusion.41
  461.4 1.7 mul.146
  463.1 1.8 reduce_sum.51
  464.9 0.9 add_rsqrt_fusion
  465.7 0.4 multiply_reduce_fusion
  466.2 0.7 copy.41
  466.9 0.2 mul.147
  467.1 0.7 fusion.21
  (48 shorter events, 1.0 us)
Async XLA Ops:
  8.0 1.6 copy-start
  8.0 4.0 copy-start.3
  8.0 43.2 %reduce-scatter.3.cloned.1.call-start = ((), (), s32[]{:S(2)}) async-start(), calls=%async_computation.4 | async-start | bytes 1179648 | tf_op jit(solution)/shard_map/reduce_scatter | solution.py:40
  11.9 39.3 %copy-start.2 = (bf16[16,2048]{1,0:T(8,128)(2,1)S(1)}, bf16[16,2048]{1,0:T(8,128)(2,1)}, u32[]{:S(2)}) copy-start(bf16[16,2048]{1,0:T(8,128)(2,1)} %param.16) | copy-start | bytes 196612
  11.9 40.4 %copy-start.5 = (f32[2048]{0:T(1024)S(1)}, f32[2048]{0:T(1024)}, u32[]{:S(2)}) copy-start(f32[2048]{0:T(1024)} %param.17) | copy-start | bytes 24580
  213.1 12.9 %copy-start.7 = (f32[128,8]{0,1:T(8,128)S(1)}, f32[128,8]{0,1:T(8,128)}, u32[]{:S(2)}) copy-start(f32[128,8]{0,1:T(8,128)} %param.19) | copy-start | bytes 12292
  213.1 114.7 %all-to-all-start.1 = ((bf16[64,12,2048]{2,1,0:T(8,128)(2,1)}), bf16[64,12,2048]{2,1,0:T(8,128)(2,1)}, u32[]{:S(2)}, u32[]{:S(2)}) async-start(bf16[64,12,2048]{2,1,0:T(8,128)(2,1)} %reshape.205), calls=%async_computation.2 | async-start | bytes 8388608 | tf_op jit(solution)/shard_map/all_to_all | solution.py:79
  225.8 198.7 %reduce-scatter.5.cloned.1.call-start = ((), (), s32[]{:S(2)}) async-start(), calls=%async_computation.5 | async-start | bytes 589824 | tf_op jit(solution)/shard_map/reduce_scatter | solution.py:86
  334.5 17.3 %copy-start.4 = (bf16[32,128]{1,0:T(8,128)(2,1)S(1)}, bf16[32,128]{1,0:T(8,128)(2,1)}, u32[]{:S(2)}) copy-start(bf16[32,128]{1,0:T(8,128)(2,1)} %param.25) | copy-start | bytes 24580
  334.5 90.0 %copy-start.9 = (f32[128]{0:T(128)S(1)}, f32[128]{0:T(128)}, u32[]{:S(2)}) copy-start(f32[128]{0:T(128)} %param.26) | copy-start | bytes 1540
  334.5 91.0 %copy-start.6 = (f32[2048]{0:T(1024)S(1)}, f32[2048]{0:T(1024)}, u32[]{:S(2)}) copy-start(f32[2048]{0:T(1024)} %param.23) | copy-start | bytes 24580
  351.1 107.4 %all-gather.2.cloned.1.call-start = ((), (), s32[]{:S(2)}) async-start(), calls=%async_computation.6 | async-start | bytes 2129920 | tf_op jit(solution)/shard_map/all_gather | solution.py:96
  424.5 41.6 %copy-start.8 = (f32[128]{0:T(128)S(1)}, f32[128]{0:T(128)}, u32[]{:S(2)}) copy-start(f32[128]{0:T(128)} %param.27) | copy-start | bytes 1540
  425.5 41.6 %copy-start.1 = (bf16[16,2048]{1,0:T(8,128)(2,1)}, bf16[16,2048]{1,0:T(8,128)(2,1)S(1)}, u32[]{:S(2)}) copy-start(bf16[16,2048]{1,0:T(8,128)(2,1)S(1)} %get-tuple-element.16) | copy-start | bytes 196612
Sparse Core Ops, SparseCore 0:
  12.1 39.1 reduce-scatter.2
  351.3 53.9 reduce-scatter.4
Sparse Core Ops, SparseCore 1:
  354.7 103.8 all-gather.1
where the time goes:
time: 476 us; the launch traced here: 475 us
  blocking collectives  211 us (44%)
  waiting for transfers between devices  149 us (31%)
  local copies, waits for them, and re-layouts  46 us (10%)
  other arithmetic  24.7 us (5%)
  between operations  15.8 us (3%)
  matrix products  15.2 us (3%)
  starting transfers between devices  12.9 us (3%)
    all_to_all x1, blocking collectives, per_device(): lax.all_to_all(outgoing, 'expert', split_axis=0, concat_axis=0, tiled=True)  112 us
    all_to_all x1, waiting for transfers between devices, per_device(): lax.all_to_all(send_part, 'expert', split_axis=0, concat_axis=0, tiled=True)  96.7 us
    all_gather x1, blocking collectives, per_device(): lax.all_gather(kv_weight, 'expert', axis=0, tiled=True)  72.7 us
    reduce_scatter x1, waiting for transfers between devices, per_device(): lax.psum_scatter(jnp.dot(attn_out, out_weight, preferred_element_type=jnp...  32 us
    all_gather x1, waiting for transfers between devices, per_device(): lax.all_gather(q_weight, 'expert', axis=0, tiled=True)  19.9 us
    scatter-add x1, other arithmetic, per_device(): term = jnp.zeros((group_rows + 1, width), jnp.float32).at[own_slots.resha...  15.8 us
    all_gather x1, blocking collectives, per_device(): group_normed = lax.all_gather(normed, 'tensor', axis=0, tiled=True)  13.8 us
    all_gather x1, blocking collectives, per_device(): next_normed = lax.all_gather(own_normed, 'tensor', axis=0, tiled=True)  13.1 us
  transfers between devices with their start and end apart: 4, of which 3 were waited for; matrix products, arithmetic and copies ran while one was open for 3% of the time, Pallas kernels for 0%

commit v1 on v0

--- a/solution.py
+++ b/solution.py
@@ -2,6 +2,7 @@
 import jax.numpy as jnp
 from jax import lax
 from jax.sharding import PartitionSpec as P
+from jax.lax import all_to_all, psum
 
 KV_HEADS = 4
 TOP = 8
@@ -96,11 +97,16 @@
         lax.all_gather(q_weight, "expert", axis=0, tiled=True),
         preferred_element_type=jnp.float32,
     )
-    kv_raw = jnp.dot(
-        next_normed,
-        lax.all_gather(kv_weight, "expert", axis=0, tiled=True),
-        preferred_element_type=jnp.float32,
+    open_pieces_all = lambda unit: jnp.concatenate(
+        all_to_all(
+            jnp.stack([unit for _ in range(psum(1, axis_name="expert"))], axis=0),
+            axis_name="expert",
+            split_axis=0,
+            concat_axis=0,
+        ),
+        axis=0,
     )
+    kv_raw = jnp.dot(next_normed, open_pieces_all(kv_weight), preferred_element_type=jnp.float32)
     head_size = q_gain.shape[0]
     queries = (
         normalize(query_raw.reshape(group_rows, -1, head_size), q_gain)

time: 476 us -> 477 us (level)
  blocking collectives: 211 us -> 139 us
  waiting for transfers between devices: 149 us -> 189 us
  starting transfers between devices: 12.9 us -> 44.3 us
    all_gather x1 -> x0, blocking collectives: 72.7 us -> none  [per_device(): lax.all_gather(kv_weight, 'expert', axis=0, tiled=True)]
    all_to_all x0 -> x1, starting transfers between devices: none -> 31.5 us  [per_device(): all_to_all(jnp.stack([unit for _ in range(psum(1, axis_name='expert'))],...]
    reduce_scatter x1, waiting for transfers between devices: 0.02 us -> 21.7 us  [per_device(): lax.psum_scatter(term.astype(jnp.bfloat16), 'tensor', scatter_dimension=0...]
    all_gather x1, waiting for transfers between devices: 19.9 us -> 38.4 us  [per_device(): lax.all_gather(q_weight, 'expert', axis=0, tiled=True)]
  transfers between devices with their start and end apart: 4 -> 5, of which waited for: 3 -> 4; matrix products, arithmetic and copies ran while one was open for 3% -> 4% of each run, Pallas kernels for 0% -> 0%
where the time goes in v1:
time: 477 us; the launch traced here: 476 us
  waiting for transfers between devices  189 us (40%)
  blocking collectives  139 us (29%)
  local copies, waits for them, and re-layouts  46.9 us (10%)
  starting transfers between devices  44.3 us (9%)
  other arithmetic  24.7 us (5%)
  between operations  15.9 us (3%)
  matrix products  15.2 us (3%)
    all_to_all x1, blocking collectives, per_device(): lax.all_to_all(outgoing, 'expert', split_axis=0, concat_axis=0, tiled=True)  112 us
    all_to_all x1, waiting for transfers between devices, per_device(): lax.all_to_all(send_part, 'expert', split_axis=0, concat_axis=0, tiled=True)  96.7 us
    all_gather x1, waiting for transfers between devices, per_device(): lax.all_gather(q_weight, 'expert', axis=0, tiled=True)  38.4 us
    reduce_scatter x1, waiting for transfers between devices, per_device(): lax.psum_scatter(jnp.dot(attn_out, out_weight, preferred_element_type=jnp...  32 us
    all_to_all x1, starting transfers between devices, per_device(): all_to_all(jnp.stack([unit for _ in range(psum(1, axis_name='expert'))],...  31.5 us
    reduce_scatter x1, waiting for transfers between devices, per_device(): lax.psum_scatter(term.astype(jnp.bfloat16), 'tensor', scatter_dimension=0...  21.7 us
    scatter-add x1, other arithmetic, per_device(): term = jnp.zeros((group_rows + 1, width), jnp.float32).at[own_slots.resha...  15.8 us
    all_gather x1, blocking collectives, per_device(): group_normed = lax.all_gather(normed, 'tensor', axis=0, tiled=True)  13.8 us
  transfers between devices with their start and end apart: 5, of which 4 were waited for; matrix products, arithmetic and copies ran while one was open for 4% of the time, Pallas kernels for 0%

profile of v1, /device:TPU:2, one launch (start us, length us, event | category | flops | bytes accessed | tf_op | source)
XLA Modules:
  0.0 475.7 jit_solution(13633351539413089812)
XLA Ops:
  8.1 1.5 copy-done
  9.6 2.3 fusion.42
  12.0 0.1 copy.34
  12.3 0.1 copy.33
  12.5 0.1 copy.36
  12.6 0.2 fusion.17
  12.9 0.1 copy.37
  13.0 0.4 fusion.16
  13.4 4.3 scatter_custom_fusion
  17.7 0.1 reshape.205
  17.9 0.5 broadcast.192
  18.4 0.7 fusion.40
  19.3 32.0 %reduce-scatter.3.cloned.1.call-done = f32[16,2048]{1,0:T(8,128)} async-done(((f32[128,2048]{1,0:T(8,128)}), f32[16,2048]{1,0:T(8,128)}) %reduce-scatter.3.cloned.1.call-update) | async-done | bytes 131088 | tf_op jit(solution)/shard_map/reduce_scatter | solution.py:41
  51.3 1.0 fusion.26
  52.4 13.8 %all_gather.9 = bf16[128,2048]{1,0:T(8,128)(2,1)S(1)} all-gather(bf16[16,2048]{1,0:T(8,128)(2,1)S(1)} %fusion.28), channel_id=1, replica_groups=mesh['expert'=64,'tensor'=8] {'tensor'}, dimensions={0}, use_global_device_ids=true | all-gather | bytes 589824 | tf_op jit(solution)/shard_map/all_gather | solution.py:49
  66.3 4.3 gather_fusion
  70.6 6.1 %reshape.214 = bf16[64,12,2048]{2,1,0:T(8,128)(2,1)} reshape(bf16[768,2048]{1,0:T(8,128)(2,1)} %gather_fusion) | data formatting | bytes 6291456 | tf_op jit(solution)/shard_map/jit(_take)/gather | solution.py:72
  76.6 2.6 broadcast_select_fusion
  79.3 111.8 %all_to_all.15 = bf16[64,12,2048]{2,1,0:T(8,128)(2,1)} all-to-all(bf16[64,12,2048]{2,1,0:T(8,128)(2,1)S(1)} %broadcast_select_fusion), channel_id=1, replica_groups=mesh['expert'=64,'tensor'=8] {'expert'}, dimensions={0} | all-to-all | bytes 6291456 | tf_op jit(solution)/shard_map/all_to_all | solution.py:73
  191.1 6.2 %reshape.209 = bf16[768,2048]{1,0:T(8,128)(2,1)} reshape(bf16[64,12,2048]{2,1,0:T(8,128)(2,1)} %all_to_all.15) | data formatting | bytes 6291456 | tf_op jit(solution)/shard_map/reshape | solution.py:74
  197.3 3.3 fusion.7
  200.5 6.5 %convolution_convert_fusion = bf16[768,2048]{1,0:T(8,128)(2,1)} fusion(bf16[768,2048]{1,0:T(8,128)(2,1)} %reshape.209, bf16[1,192,2048]{2,1,0:T(8,128)(2,1)} %param.22, bf16[1,2048,192]{1,2,0:T(8,128)(2,1)} %param.21, f32[768,192]{0,1:T(8,128)S(1)} %fusion.7), kind=kOutput, calls=%fused_computation.7 | convolution fusion | flops 1210417152 | bytes 8454144 | tf_op jit(solution)/shard_map/dot_general | solution.py:78
  207.0 6.1 %reshape.210 = bf16[64,12,2048]{2,1,0:T(8,128)(2,1)} reshape(bf16[768,2048]{1,0:T(8,128)(2,1)} %convolution_convert_fusion) | data formatting | bytes 6291456 | tf_op jit(solution)/shard_map/reshape | solution.py:79
  213.1 12.7 %all-to-all-start.1 = ((bf16[64,12,2048]{2,1,0:T(8,128)(2,1)}), bf16[64,12,2048]{2,1,0:T(8,128)(2,1)}, u32[]{:S(2)}, u32[]{:S(2)}) async-start(bf16[64,12,2048]{2,1,0:T(8,128)(2,1)} %reshape.210), calls=%async_computation.2 | async-start | bytes 8388608 | tf_op jit(solution)/shard_map/all_to_all | solution.py:80
  225.9 0.1 reshape.206
  226.0 0.1 copy.38
  226.2 4.5 scatter_custom_fusion.1
  230.7 0.1 reshape.208
  230.9 0.1 dynamic-slice_reduce_fusion
  231.1 96.7 %all-to-all-done.1 = bf16[64,12,2048]{2,1,0:T(8,128)(2,1)} async-done(((bf16[64,12,2048]{2,1,0:T(8,128)(2,1)}), bf16[64,12,2048]{2,1,0:T(8,128)(2,1)}, u32[]{:S(2)}, u32[]{:S(2)}) %all-to-all-start.1) | async-done | bytes 3145760 | tf_op jit(solution)/shard_map/all_to_all | solution.py:80
  327.8 6.7 %reshape.212 = f32[768,2048]{1,0:T(8,128)} reshape(bf16[64,12,2048]{2,1,0:T(8,128)(2,1)} %all-to-all-done.1) | data formatting | bytes 9437184 | tf_op jit(solution)/shard_map/convert_element_type | solution.py:81
  334.5 15.8 %scatter_custom_fusion.2 = f32[129,2048]{1,0:T(8,128)S(1)} fusion(s32[768]{0:T(1024)S(1)} %fusion.37, f32[768,2048]{1,0:T(8,128)} %reshape.212, f32[768]{0:T(1024)S(1)} %mul.130, f32[]{:T(128)} %constant.76.clone.1), kind=kCustom, calls=%fused_computation.4 | custom fusion | flops 3145728 | bytes 7352324 | tf_op jit(solution)/shard_map/scatter-add | solution.py:85
  350.3 0.9 slice.20
  351.2 0.5 all-gather.2.cloned.1.call-update
  351.8 0.9 stack.2
  352.6 31.5 %all-to-all-start.2 = ((bf16[64,32,128]{2,1,0:T(8,128)(2,1)}), bf16[64,32,128]{2,1,0:T(8,128)(2,1)S(1)}, u32[]{:S(2)}, u32[]{:S(2)}) async-start(bf16[64,32,128]{2,1,0:T(8,128)(2,1)} %stack.2), calls=%async_computation.4 | async-start | bytes 1048576 | tf_op jit(solution)/shard_map/all_to_all | solution.py:101
  384.1 21.7 %reduce-scatter.5.cloned.1.call-done = bf16[16,2048]{1,0:T(8,128)(2,1)} async-done(((bf16[128,2048]{1,0:T(8,128)(2,1)}), bf16[16,2048]{1,0:T(8,128)(2,1)}) %reduce-scatter.5.cloned.1.call-update) | async-done | bytes 65552 | tf_op jit(solution)/shard_map/reduce_scatter | solution.py:87
  405.8 1.0 fusion.23
  406.9 13.7 %all_gather.10 = bf16[128,2048]{1,0:T(8,128)(2,1)S(1)} all-gather(bf16[16,2048]{1,0:T(8,128)(2,1)S(1)} %fusion.25), channel_id=1, replica_groups=mesh['expert'=64,'tensor'=8] {'tensor'}, dimensions={0}, use_global_device_ids=true | all-gather | bytes 589824 | tf_op jit(solution)/shard_map/all_gather | solution.py:92
  420.6 38.4 %all-gather.2.cloned.1.call-done = bf16[2048,512]{1,0:T(8,128)(2,1)} async-done(((bf16[32,512]{1,0:T(8,128)(2,1)}), bf16[2048,512]{1,0:T(8,128)(2,1)}) %all-gather.2.cloned.1.call-update) | async-done | bytes 2097168 | tf_op jit(solution)/shard_map/all_gather | solution.py:97
  459.1 2.7 fusion.41
  461.8 1.7 mul.146
  463.5 1.8 reduce_sum.51
  465.3 0.9 add_rsqrt_fusion
  466.2 0.4 multiply_reduce_fusion
  466.7 0.7 copy.41
  467.4 0.2 mul.147
  467.6 0.7 fusion.21
  (50 shorter events, 1.2 us)
Async XLA Ops:
  8.0 1.6 copy-start
  8.0 4.0 copy-start.3
  8.0 43.2 %reduce-scatter.3.cloned.1.call-start = ((), (), s32[]{:S(2)}) async-start(), calls=%async_computation.5 | async-start | bytes 1179648 | tf_op jit(solution)/shard_map/reduce_scatter | solution.py:41
  11.9 39.3 %copy-start.2 = (bf16[16,2048]{1,0:T(8,128)(2,1)S(1)}, bf16[16,2048]{1,0:T(8,128)(2,1)}, u32[]{:S(2)}) copy-start(bf16[16,2048]{1,0:T(8,128)(2,1)} %param.16) | copy-start | bytes 196612
  11.9 40.4 %copy-start.5 = (f32[2048]{0:T(1024)S(1)}, f32[2048]{0:T(1024)}, u32[]{:S(2)}) copy-start(f32[2048]{0:T(1024)} %param.17) | copy-start | bytes 24580
  213.1 12.9 %copy-start.7 = (f32[128,8]{0,1:T(8,128)S(1)}, f32[128,8]{0,1:T(8,128)}, u32[]{:S(2)}) copy-start(f32[128,8]{0,1:T(8,128)} %param.19) | copy-start | bytes 12292
  213.1 114.7 %all-to-all-start.1 = ((bf16[64,12,2048]{2,1,0:T(8,128)(2,1)}), bf16[64,12,2048]{2,1,0:T(8,128)(2,1)}, u32[]{:S(2)}, u32[]{:S(2)}) async-start(bf16[64,12,2048]{2,1,0:T(8,128)(2,1)} %reshape.210), calls=%async_computation.2 | async-start | bytes 8388608 | tf_op jit(solution)/shard_map/all_to_all | solution.py:80
  225.8 180.0 %reduce-scatter.5.cloned.1.call-start = ((), (), s32[]{:S(2)}) async-start(), calls=%async_computation.6 | async-start | bytes 589824 | tf_op jit(solution)/shard_map/reduce_scatter | solution.py:87
  334.5 17.3 %copy-start.4 = (bf16[32,128]{1,0:T(8,128)(2,1)S(1)}, bf16[32,128]{1,0:T(8,128)(2,1)}, u32[]{:S(2)}) copy-start(bf16[32,128]{1,0:T(8,128)(2,1)} %param.25) | copy-start | bytes 24580
  350.2 33.9 %copy-start.9 = (f32[128]{0:T(128)S(1)}, f32[128]{0:T(128)}, u32[]{:S(2)}) copy-start(f32[128]{0:T(128)} %param.26) | copy-start | bytes 1540
  350.3 56.6 %copy-start.6 = (f32[2048]{0:T(1024)S(1)}, f32[2048]{0:T(1024)}, u32[]{:S(2)}) copy-start(f32[2048]{0:T(1024)} %param.23) | copy-start | bytes 24580
  351.2 107.9 %all-gather.2.cloned.1.call-start = ((), (), s32[]{:S(2)}) async-start(), calls=%async_computation.7 | async-start | bytes 2129920 | tf_op jit(solution)/shard_map/all_gather | solution.py:97
  352.6 113.6 %all-to-all-start.2 = ((bf16[64,32,128]{2,1,0:T(8,128)(2,1)}), bf16[64,32,128]{2,1,0:T(8,128)(2,1)S(1)}, u32[]{:S(2)}, u32[]{:S(2)}) async-start(bf16[64,32,128]{2,1,0:T(8,128)(2,1)} %stack.2), calls=%async_computation.4 | async-start | bytes 1048576 | tf_op jit(solution)/shard_map/all_to_all | solution.py:101
  384.1 82.5 %copy-start.8 = (f32[128]{0:T(128)S(1)}, f32[128]{0:T(128)}, u32[]{:S(2)}) copy-start(f32[128]{0:T(128)} %param.27) | copy-start | bytes 1540
  406.8 60.8 %copy-start.1 = (bf16[16,2048]{1,0:T(8,128)(2,1)}, bf16[16,2048]{1,0:T(8,128)(2,1)S(1)}, u32[]{:S(2)}) copy-start(bf16[16,2048]{1,0:T(8,128)(2,1)S(1)} %get-tuple-element.16) | copy-start | bytes 196612
Sparse Core Ops, SparseCore 0:
  12.1 39.1 reduce-scatter.2
  351.3 54.4 reduce-scatter.4
Sparse Core Ops, SparseCore 1:
  354.7 104.3 all-gather.1
